TPU v7x, 256 devices: a whole 4x4x8 slice. The times are simulated.
256 devices in a mesh: rep: 16 (over y_lo, z), tp: 16 (over x, y_hi, core).
Axes of the slice: x: 4, y: 4 (y_hi: 2, y_lo: 2; y = y_hi * 2 + y_lo), z: 8, core: 2. Of those that a mesh axis runs over, the one named last changes fastest.
Arguments:
- tokens: bfloat16 [16384, 8192], P('rep', 'tp'), may hold values from -6 to 6
- grad_out: bfloat16 [16384, 4096], P('rep', 'tp'), may hold values from -0.046875 to 0.046875
- lengths: int32 [16, 16], replicated, may hold values from 0 to 256, as said below
- master: float32 [8192, 2048], P('rep', 'tp'), may hold values from -3 to 3
- first: float32 [8192, 2048], P('rep', 'tp'), may hold values from -6 to 6
- second: float32 [8192, 2048], P('rep', 'tp'), may hold values from 0.25 to 4
Outputs:
- new_master: float32 [8192, 2048], P('rep', 'tp')
- new_first: float32 [8192, 2048], P('rep', 'tp')
- new_second: float32 [8192, 2048], P('rep', 'tp')
- healthy_weights: bfloat16 [8192, 2048], P(None, 'tp')
- slot_weights: bfloat16 [16, 8192, 4096], P('rep', None, 'tp')
Inputs may be any that keep to these rules, and one draw needn't show every extreme that they name: `lengths`: each row is one replica's split of the 2048 columns over its devices in tp order: the entries are multiples of 64, sum to 2048, the nonzero ones come first and number at least half of the row; a row is either all 128 or has an entry equal to 256, and some row has an entry equal to 256.
All inputs are finite; a program needn't handle non-finite values.
Results may differ from a plain program's by a relative error of at most 0.0019.
Values may be sent and summed in bfloat16 or wider, within the bound.
No kernel may reach another device: no remote copies, remote signals or barrier semaphores. Data moves between devices by JAX's collectives and lax.ppermute only.
A program may use at most 128 MiB of HBM per device.

v0:
```python
import jax
import jax.numpy as jnp
from jax import lax
from jax.sharding import Mesh
from jax.sharding import PartitionSpec as P

COLS = 2048
STEP = 1000
REP = ("rep_0", "rep_1")
decay_first = 0.9
decay_second = 0.999
learning_rate = 0.02
weight_decay = 0.1
epsilon = 1e-08


def own_block(parts, axes, turns):
    inside = parts.shape[1:]
    parts = parts.reshape(*(lax.axis_size(a) for a in axes), *inside)
    parts = jnp.moveaxis(parts, turns, range(len(axes))).reshape(-1, *inside)
    for k in turns:
        parts = lax.psum_scatter(parts, axes[k], scatter_dimension=0, tiled=True)
    return parts[0]


def in_blocks(value, dim, size):
    before, after = (value.shape[:dim], value.shape[dim + 1 :])
    return jnp.moveaxis(value.reshape(*before, size, -1, *after), dim, 0)


def summed_rows(value, axes, turns, dim):
    size = lax.axis_size(axes)
    return own_block(in_blocks(value, dim, size), axes, turns)


def from_everyone(value, axis):
    copies = jnp.broadcast_to(value, (lax.axis_size(axis), *value.shape))
    return lax.all_to_all(copies, axis, split_axis=0, concat_axis=0, tiled=True)


def laid_out(parts, dim):
    shape = list(parts.shape[1:])
    shape[dim] *= parts.shape[0]
    return jnp.moveaxis(parts, 0, dim).reshape(shape)


def gathered_copies(value, axis, dim):
    parts = from_everyone(value, axis)
    return laid_out(parts, dim)


def adam_update(master, first, second, gradient):
    scale_first = 1.0 - decay_first**STEP
    scale_second = 1.0 - decay_second**STEP
    new_first = decay_first * first + (1.0 - decay_first) * gradient
    new_second = decay_second * second + (1.0 - decay_second) * gradient * gradient
    direction = new_first / scale_first / (jnp.sqrt(new_second / scale_second) + epsilon)
    new_master = master - learning_rate * (direction + weight_decay * master)
    return (new_master, new_first, new_second)


def on_device(tokens, grad_out, lengths, master, first, second):
    shards = lax.axis_size("tp")
    replicas = lax.axis_size(REP)
    column_index = lax.axis_index("tp")
    replica_index = lax.axis_index(REP)
    token_count = tokens.shape[0]
    slot_width = grad_out.shape[1]
    block_width = COLS // shards
    begins_all = jnp.cumsum(lengths, axis=1) - lengths
    is_mine = jnp.arange(shards, dtype=jnp.int32) == column_index
    own_lengths = lax.dynamic_index_in_dim(lengths, replica_index, 0, keepdims=False)
    own_begins = lax.dynamic_index_in_dim(begins_all, replica_index, 0, keepdims=False)
    my_begin = jnp.sum(jnp.where(is_mine, own_begins, 0))
    my_length = jnp.sum(jnp.where(is_mine, own_lengths, 0))
    columns = jnp.arange(COLS, dtype=jnp.int32)
    offset = columns - my_begin
    inside = (offset >= 0) & (offset < my_length)
    picked = jnp.take(grad_out, jnp.clip(offset, 0, slot_width - 1), axis=1)
    spread = jnp.where(inside[None, :], picked, jnp.zeros_like(picked)).reshape(
        token_count, shards, block_width
    )
    received = lax.all_to_all(spread, "tp", split_axis=1, concat_axis=1, tiled=True)
    grad_block = jnp.sum(received, axis=1)
    grad_columns = lax.dot_general(
        lax.all_gather(tokens, "tp", axis=1, tiled=True),
        grad_block,
        (((0,), (0,)), ((), ())),
        preferred_element_type=jnp.float32,
    )
    summed = summed_rows(grad_columns.astype(jnp.bfloat16), REP, (1, 0), 0).astype(jnp.float32)
    new_master, new_first, new_second = adam_update(master, first, second, summed)
    weights = new_master.astype(jnp.bfloat16)
    healthy = gathered_copies(weights, REP, 0)
    replica_rows = lax.all_gather(weights, "tp", axis=1, tiled=True)
    slot_begins = jnp.sum(jnp.where(is_mine[None, :], begins_all, 0), axis=1)
    slot_lengths = jnp.sum(jnp.where(is_mine[None, :], lengths, 0), axis=1)
    within = jnp.arange(slot_width, dtype=jnp.int32)
    source_cols = slot_begins[:, None] + within[None, :]
    valid = within[None, :] < slot_lengths[:, None]
    taken = jnp.take(replica_rows, jnp.clip(source_cols, 0, COLS - 1).reshape(-1), axis=1)
    outgoing = jnp.where(valid.reshape(-1)[None, :], taken, jnp.zeros_like(taken))
    outgoing = outgoing.reshape(replica_rows.shape[0], replicas, slot_width)
    arrived = lax.all_to_all(outgoing, REP, split_axis=1, concat_axis=0, tiled=True)
    slot_weights = arrived.reshape(1, -1, slot_width)
    return (new_master, new_first, new_second, healthy, slot_weights)


def solution(mesh):
    torus = Mesh(mesh.devices.reshape(2, 8, mesh.shape["tp"]), ("rep_0", "rep_1", "tp"))
    placed = (P(REP, "tp"), P(REP, "tp"), P(), P(REP, "tp"), P(REP, "tp"), P(REP, "tp"))
    return jax.shard_map(
        on_device,
        mesh=torus,
        in_specs=placed,
        out_specs=(P(REP, "tp"), P(REP, "tp"), P(REP, "tp"), P(None, "tp"), P(REP, None, "tp")),
        check_vma=False,
    )
```

profile of v0, /device:TPU:32, one launch (start us, length us, event | category | flops | bytes accessed | tf_op | source)
XLA Modules:
  0.0 450.8 jit_solution(10688095374911271748)
XLA Ops:
  7.2 0.7 all-gather.3.cloned.1.call-update
  8.0 0.9 reduce_window_sum.11
  8.8 1.2 copy.34
  10.1 0.8 select_reduce_fusion.1
  10.9 1.3 fusion.12
  12.2 0.7 compare_select_fusion.1
  12.9 9.6 %gather_fusion = bf16[2048,1024]{1,0:T(8,128)(2,1)} fusion(bf16[1024,256]{0,1:T(8,128)(2,1)S(1)} %copy.34, s32[2048]{0:T(1024)S(1)} %broadcast_clamp_fusion.1), kind=kCustom, calls=%fused_computation | custom fusion | bytes 8396800 | tf_op jit(solution)/shard_map/jit(_take)/gather | solution.py:79
  22.5 0.7 fusion.10
  23.2 1.3 fusion.11
  24.5 3.1 select_select_fusion.1
  27.6 73.9 %all_to_all.25 = bf16[1024,16,128]{0,2,1:T(8,128)(2,1)} all-to-all(bf16[1024,16,128]{0,2,1:T(8,128)(2,1)S(1)} %select_select_fusion.1), channel_id=1, replica_groups=mesh['rep_0'=2,'rep_1'=8,'tp'=16] {'tp'}, dimensions={1} | all-to-all | bytes 8388608 | tf_op jit(solution)/shard_map/all_to_all | solution.py:83
  101.5 3.1 reduce_sum.50
  104.7 63.9 %all-gather.3.cloned.1.call-done = bf16[1024,8192]{1,0:T(8,128)(2,1)} async-done(((bf16[1024,512]{1,0:T(8,128)(2,1)}), bf16[1024,8192]{1,0:T(8,128)(2,1)}) %all-gather.3.cloned.1.call-update) | async-done | bytes 16777232 | tf_op jit(solution)/shard_map/all_gather | solution.py:86
  168.6 8.1 %convolution_convert_fusion = bf16[128,8192]{1,0:T(8,128)(2,1)S(1)} fusion(bf16[1024,128]{0,1:T(8,128)(2,1)S(1)} %reduce_sum.50, bf16[1024,8192]{1,0:T(8,128)(2,1)} %all-gather.3.cloned.1.call-done), kind=kOutput, calls=%fused_computation.2 | convolution fusion | flops 2148532224 | bytes 19136512 | tf_op jit(solution)/shard_map/dot_general | solution.py:85
  176.7 0.9 copy.44
  177.6 2.5 copy.35
  180.2 41.0 %reduce-scatter.3.cloned.1.call-done = bf16[2,512,128]{1,2,0:T(8,128)(2,1)} async-done(((bf16[16,512,128]{1,2,0:T(8,128)(2,1)}), bf16[2,512,128]{1,2,0:T(8,128)(2,1)}) %reduce-scatter.3.cloned.1.call-update) | async-done | bytes 262160 | tf_op jit(solution)/shard_map/reduce_scatter | solution.py:22
  221.7 18.0 %reduce-scatter.5.cloned.1.call-done = bf16[1,512,128]{1,2,0:T(8,128)(2,1)} async-done(((bf16[2,512,128]{1,2,0:T(8,128)(2,1)}), bf16[1,512,128]{1,2,0:T(8,128)(2,1)}) %reduce-scatter.5.cloned.1.call-update) | async-done | bytes 131088 | tf_op jit(solution)/shard_map/reduce_scatter | solution.py:22
  239.7 1.8 fusion.14
  241.5 1.0 copy.39
  242.5 1.7 broadcast_in_dim.78
  244.3 7.5 %all-to-all-start.1 = ((bf16[16,512,128]{2,1,0:T(8,128)(2,1)}), bf16[16,512,128]{2,1,0:T(8,128)(2,1)S(1)}, u32[]{:S(2)}, u32[]{:S(2)}) async-start(bf16[16,512,128]{2,1,0:T(8,128)(2,1)} %broadcast_in_dim.78), calls=%async_computation.3 | async-start | bytes 4194304 | tf_op jit(solution)/shard_map/all_to_all | solution.py:38
  252.0 52.9 %all-gather.5.cloned.1.call-done = bf16[512,2048]{0,1:T(8,128)(2,1)} async-done(((bf16[512,128]{0,1:T(8,128)(2,1)}), bf16[512,2048]{0,1:T(8,128)(2,1)}) %all-gather.5.cloned.1.call-update) | async-done | bytes 2097168 | tf_op jit(solution)/shard_map/all_gather | solution.py:95
  304.9 19.3 %gather_fusion.1 = bf16[4096,512]{1,0:T(8,128)(2,1)} fusion(bf16[512,2048]{0,1:T(8,128)(2,1)} %all-gather.5.cloned.1.call-done, s32[4096]{0:T(1024)S(1)} %broadcast_clamp_fusion), kind=kCustom, calls=%fused_computation.1 | custom fusion | bytes 8404992 | tf_op jit(solution)/shard_map/jit(_take)/gather | solution.py:101
  324.2 5.2 %select_select_fusion = bf16[512,16,256]{0,2,1:T(8,128)(2,1)} fusion(bf16[512,16,256]{0,2,1:T(8,128)(2,1)} %bitcast.43, pred[16,256]{1,0:T(8,128)(4,1)S(1)} %get-tuple-element.30, pred[16,256]{1,0:T(8,128)(4,1)S(1)} %get-tuple-element.29), kind=kLoop, calls=%fused_computation.3 | loop fusion | flops 4194304 | bytes 8396800 | tf_op jit(solution)/shard_map/jit(_where)/select_n | solution.py:102
  329.5 11.3 %all-to-all-start.2 = ((bf16[512,16,256]{0,2,1:T(8,128)(2,1)}), bf16[512,16,256]{0,2,1:T(8,128)(2,1)}, u32[]{:S(2)}, u32[]{:S(2)}) async-start(bf16[512,16,256]{0,2,1:T(8,128)(2,1)} %select_select_fusion), calls=%async_computation.4 | async-start | bytes 8388608 | tf_op jit(solution)/shard_map/all_to_all | solution.py:104
  340.7 0.8 copy.41
  341.6 0.8 copy.42
  342.4 0.8 copy.43
  343.2 93.3 %all-to-all-done.2 = bf16[512,16,256]{0,2,1:T(8,128)(2,1)} async-done(((bf16[512,16,256]{0,2,1:T(8,128)(2,1)}), bf16[512,16,256]{0,2,1:T(8,128)(2,1)}, u32[]{:S(2)}, u32[]{:S(2)}) %all-to-all-start.2) | async-done | bytes 4194336 | tf_op jit(solution)/shard_map/all_to_all | solution.py:104
  436.6 6.4 %copy.40 = bf16[16,512,1,256]{3,1,0,2:T(8,128)(2,1)} copy(bf16[16,512,1,256]{1,3,0,2:T(8,128)(2,1)} %bitcast.15) | data formatting | bytes 8388608 | tf_op jit(solution)/shard_map/all_to_all | solution.py:104
  443.0 1.3 copy.47
  (24 shorter events, 0.8 us)
Async XLA Ops:
  7.2 161.4 %all-gather.3.cloned.1.call-start = ((), (), s32[]{:S(2)}) async-start(), calls=%async_computation.5 | async-start | bytes 17825792 | tf_op jit(solution)/shard_map/all_gather | solution.py:86
  7.9 213.3 %reduce-scatter.3.cloned.1.call-start = ((), (), s32[]{:S(2)}) async-start(), calls=%async_computation.6 | async-start | bytes 2359296 | tf_op jit(solution)/shard_map/reduce_scatter | solution.py:22
  177.6 43.7 %copy-start = (f32[512,128]{1,0:T(8,128)S(1)}, f32[512,128]{1,0:T(8,128)}, u32[]{:S(2)}) copy-start(f32[512,128]{1,0:T(8,128)} %param.10) | copy-start | bytes 786436
  177.6 43.8 %copy-start.1 = (f32[512,128]{1,0:T(8,128)S(1)}, f32[512,128]{1,0:T(8,128)}, u32[]{:S(2)}) copy-start(f32[512,128]{1,0:T(8,128)} %param.11) | copy-start | bytes 786436
  177.6 43.9 %copy-start.2 = (f32[512,128]{1,0:T(8,128)S(1)}, f32[512,128]{1,0:T(8,128)}, u32[]{:S(2)}) copy-start(f32[512,128]{1,0:T(8,128)} %param.9) | copy-start | bytes 786436
  180.1 59.6 %reduce-scatter.5.cloned.1.call-start = ((), (), s32[]{:S(2)}) async-start(), calls=%async_computation.7 | async-start | bytes 393216 | tf_op jit(solution)/shard_map/reduce_scatter | solution.py:22
  221.2 83.7 %all-gather.5.cloned.1.call-start = ((), (), s32[]{:S(2)}) async-start(), calls=%async_computation.8 | async-start | bytes 2228224 | tf_op jit(solution)/shard_map/all_gather | solution.py:95
  244.3 85.2 %all-to-all-start.1 = ((bf16[16,512,128]{2,1,0:T(8,128)(2,1)}), bf16[16,512,128]{2,1,0:T(8,128)(2,1)S(1)}, u32[]{:S(2)}, u32[]{:S(2)}) async-start(bf16[16,512,128]{2,1,0:T(8,128)(2,1)} %broadcast_in_dim.78), calls=%async_computation.3 | async-start | bytes 4194304 | tf_op jit(solution)/shard_map/all_to_all | solution.py:38
  329.5 107.1 %all-to-all-start.2 = ((bf16[512,16,256]{0,2,1:T(8,128)(2,1)}), bf16[512,16,256]{0,2,1:T(8,128)(2,1)}, u32[]{:S(2)}, u32[]{:S(2)}) async-start(bf16[512,16,256]{0,2,1:T(8,128)(2,1)} %select_select_fusion), calls=%async_computation.4 | async-start | bytes 8388608 | tf_op jit(solution)/shard_map/all_to_all | solution.py:104
Sparse Core Ops, SparseCore 0:
  10.5 158.0 all-gather.2
  180.3 40.8 reduce-scatter.2
  223.7 16.0 reduce-scatter.4
  242.8 62.0 all-gather.4
where the time goes:
time: 452 us; the launch traced here: 451 us
  waiting for transfers between devices  270 us (60%)
  blocking collectives  73.9 us (16%)
  local copies, waits for them, and re-layouts  46.9 us (10%)
  other arithmetic  19.1 us (4%)
  starting transfers between devices  18.9 us (4%)
  between operations  13.9 us (3%)
  matrix products  8.12 us (2%)
    all_to_all x1, waiting for transfers between devices, on_device(): lax.all_to_all(outgoing, REP, split_axis=1, concat_axis=0, tiled=True)  93.3 us
    all_to_all x1, blocking collectives, on_device(): lax.all_to_all(spread, 'tp', split_axis=1, concat_axis=1, tiled=True)  73.9 us
    all_gather x1, waiting for transfers between devices, on_device(): lax.all_gather(tokens, 'tp', axis=1, tiled=True)  63.9 us
    reduce_scatter x2, waiting for transfers between devices, own_block(): parts = lax.psum_scatter(parts, axes[k], scatter_dimension=0, tiled=True)  59 us
    all_gather x1, waiting for transfers between devices, on_device(): replica_rows = lax.all_gather(weights, 'tp', axis=1, tiled=True)  52.9 us
    gather x1, local copies, waits for them, and re-layouts, on_device(): jnp.take(replica_rows, jnp.clip(source_cols, 0, COLS - 1).reshape(-1), ax...  19.3 us
    all_to_all x1, starting transfers between devices, on_device(): lax.all_to_all(outgoing, REP, split_axis=1, concat_axis=0, tiled=True)  11.3 us
    gather x1, local copies, waits for them, and re-layouts, on_device(): picked = jnp.take(grad_out, jnp.clip(offset, 0, slot_width - 1), axis=1)  9.61 us
  transfers between devices with their start and end apart: 6, of which 5 were waited for; matrix products, arithmetic and copies ran while one was open for 12% of the time, Pallas kernels for 0%

commit v1 on v0

--- a/solution.py
+++ b/solution.py
@@ -3,6 +3,7 @@
 from jax import lax
 from jax.sharding import Mesh
 from jax.sharding import PartitionSpec as P
+from jax.lax import all_gather
 
 COLS = 2048
 STEP = 1000
@@ -92,7 +93,8 @@
     new_master, new_first, new_second = adam_update(master, first, second, summed)
     weights = new_master.astype(jnp.bfloat16)
     healthy = gathered_copies(weights, REP, 0)
-    replica_rows = lax.all_gather(weights, "tp", axis=1, tiled=True)
+    enter_the_keys = lambda xs: jnp.concatenate(all_gather(xs, "tp"), 1)
+    replica_rows = enter_the_keys(weights)
     slot_begins = jnp.sum(jnp.where(is_mine[None, :], begins_all, 0), axis=1)
     slot_lengths = jnp.sum(jnp.where(is_mine[None, :], lengths, 0), axis=1)
     within = jnp.arange(slot_width, dtype=jnp.int32)

time: 452 us -> 455 us (level)
  transfers between devices with their start and end apart: 6 -> 6, of which waited for: 5 -> 5; matrix products, arithmetic and copies ran while one was open for 12% -> 11% of each run, Pallas kernels for 0% -> 0%
where the time goes in v1:
time: 455 us; the launch traced here: 454 us
  waiting for transfers between devices  273 us (60%)
  blocking collectives  73.9 us (16%)
  local copies, waits for them, and re-layouts  47 us (10%)
  other arithmetic  19.3 us (4%)
  starting transfers between devices  18.9 us (4%)
  between operations  13.9 us (3%)
  matrix products  8.12 us (2%)
    all_to_all x1, waiting for transfers between devices, on_device(): lax.all_to_all(outgoing, REP, split_axis=1, concat_axis=0, tiled=True)  95.9 us
    all_to_all x1, blocking collectives, on_device(): lax.all_to_all(spread, 'tp', split_axis=1, concat_axis=1, tiled=True)  73.9 us
    all_gather x1, waiting for transfers between devices, on_device(): lax.all_gather(tokens, 'tp', axis=1, tiled=True)  63.9 us
    reduce_scatter x2, waiting for transfers between devices, own_block(): parts = lax.psum_scatter(parts, axes[k], scatter_dimension=0, tiled=True)  59.5 us
    all_gather x1, waiting for transfers between devices, on_device(): enter_the_keys = lambda xs: jnp.concatenate(all_gather(xs, 'tp'), 1)  52.9 us
    gather x1, local copies, waits for them, and re-layouts, on_device(): jnp.take(replica_rows, jnp.clip(source_cols, 0, COLS - 1).reshape(-1), ax...  17.3 us
    all_to_all x1, starting transfers between devices, on_device(): lax.all_to_all(outgoing, REP, split_axis=1, concat_axis=0, tiled=True)  11.3 us
    gather x1, local copies, waits for them, and re-layouts, on_device(): picked = jnp.take(grad_out, jnp.clip(offset, 0, slot_width - 1), axis=1)  9.61 us
  transfers between devices with their start and end apart: 6, of which 5 were waited for; matrix products, arithmetic and copies ran while one was open for 11% of the time, Pallas kernels for 0%

profile of v1, /device:TPU:32, one launch (start us, length us, event | category | flops | bytes accessed | tf_op | source)
XLA Modules:
  0.0 454.0 jit_solution(642402272988602176)
XLA Ops:
  7.2 0.7 all-gather.4.cloned.1.call-update
  8.0 0.9 reduce_window_sum.11
  8.8 1.2 copy.19
  10.1 0.8 select_reduce_fusion.1
  10.9 1.3 fusion.12
  12.2 0.7 compare_select_fusion.1
  12.9 9.6 %gather_fusion = bf16[2048,1024]{1,0:T(8,128)(2,1)} fusion(bf16[1024,256]{0,1:T(8,128)(2,1)S(1)} %copy.19, s32[2048]{0:T(1024)S(1)} %broadcast_clamp_fusion.1), kind=kCustom, calls=%fused_computation | custom fusion | bytes 8396800 | tf_op jit(solution)/shard_map/jit(_take)/gather | solution.py:80
  22.5 0.7 fusion.10
  23.2 1.3 fusion.11
  24.5 3.1 select_select_fusion.1
  27.6 73.9 %all_to_all.25 = bf16[1024,16,128]{0,2,1:T(8,128)(2,1)} all-to-all(bf16[1024,16,128]{0,2,1:T(8,128)(2,1)S(1)} %select_select_fusion.1), channel_id=1, replica_groups=mesh['rep_0'=2,'rep_1'=8,'tp'=16] {'tp'}, dimensions={1} | all-to-all | bytes 8388608 | tf_op jit(solution)/shard_map/all_to_all | solution.py:84
  101.5 3.1 reduce_sum.50
  104.7 63.9 %all-gather.4.cloned.1.call-done = bf16[1024,8192]{1,0:T(8,128)(2,1)} async-done(((bf16[1024,512]{1,0:T(8,128)(2,1)}), bf16[1024,8192]{1,0:T(8,128)(2,1)}) %all-gather.4.cloned.1.call-update) | async-done | bytes 16777232 | tf_op jit(solution)/shard_map/all_gather | solution.py:87
  168.6 8.1 %convolution_convert_fusion = bf16[128,8192]{1,0:T(8,128)(2,1)S(1)} fusion(bf16[1024,128]{0,1:T(8,128)(2,1)S(1)} %reduce_sum.50, bf16[1024,8192]{1,0:T(8,128)(2,1)} %all-gather.4.cloned.1.call-done), kind=kOutput, calls=%fused_computation.2 | convolution fusion | flops 2148532224 | bytes 19136512 | tf_op jit(solution)/shard_map/dot_general | solution.py:86
  176.7 0.9 copy.23
  177.6 3.0 copy.20
  180.7 0.0 reduce-scatter.5.cloned.1.call-start
  180.7 41.0 %reduce-scatter.3.cloned.1.call-done = bf16[2,512,128]{2,1,0:T(8,128)(2,1)} async-done(((bf16[16,512,128]{2,1,0:T(8,128)(2,1)}), bf16[2,512,128]{2,1,0:T(8,128)(2,1)}) %reduce-scatter.3.cloned.1.call-update) | async-done | bytes 262160 | tf_op jit(solution)/shard_map/reduce_scatter | solution.py:23
  221.8 18.5 %reduce-scatter.5.cloned.1.call-done = bf16[1,512,128]{2,1,0:T(8,128)(2,1)} async-done(((bf16[2,512,128]{2,1,0:T(8,128)(2,1)}), bf16[1,512,128]{2,1,0:T(8,128)(2,1)}) %reduce-scatter.5.cloned.1.call-update) | async-done | bytes 131088 | tf_op jit(solution)/shard_map/reduce_scatter | solution.py:23
  240.3 1.9 fusion.14
  242.2 2.6 broadcast_in_dim.78
  244.9 7.5 %all-to-all-start.1 = ((bf16[16,512,128]{2,1,0:T(8,128)(2,1)}), bf16[16,512,128]{2,1,0:T(8,128)(2,1)}, u32[]{:S(2)}, u32[]{:S(2)}) async-start(bf16[16,512,128]{2,1,0:T(8,128)(2,1)} %broadcast_in_dim.78), calls=%async_computation.3 | async-start | bytes 4194304 | tf_op jit(solution)/shard_map/all_to_all | solution.py:39
  252.4 0.1 fusion.2
  252.5 0.1 iota_compare_fusion
  252.6 52.9 %all-gather.6.cloned.1.call-done = bf16[8192,128]{1,0:T(8,128)(2,1)} async-done(((bf16[512,128]{1,0:T(8,128)(2,1)}), bf16[8192,128]{1,0:T(8,128)(2,1)}) %all-gather.6.cloned.1.call-update) | async-done | bytes 2097168 | tf_op jit(solution)/shard_map/all_gather | solution.py:96
  305.5 2.9 copy.21
  308.4 17.3 %gather_fusion.1 = bf16[4096,512]{1,0:T(8,128)(2,1)} fusion(bf16[512,2048]{0,1:T(8,128)(2,1)S(1)} %bitcast.47, s32[4096]{0:T(1024)S(1)} %broadcast_clamp_fusion), kind=kCustom, calls=%fused_computation.1 | custom fusion | bytes 8404992 | tf_op jit(solution)/shard_map/jit(_take)/gather | solution.py:103
  325.7 5.2 %select_select_fusion = bf16[512,16,256]{0,2,1:T(8,128)(2,1)} fusion(bf16[512,16,256]{0,2,1:T(8,128)(2,1)} %bitcast.48, pred[16,256]{1,0:T(8,128)(4,1)S(1)} %get-tuple-element.15, pred[16,256]{1,0:T(8,128)(4,1)S(1)} %get-tuple-element.14), kind=kLoop, calls=%fused_computation.3 | loop fusion | flops 4194304 | bytes 8396800 | tf_op jit(solution)/shard_map/jit(_where)/select_n | solution.py:104
  331.0 11.3 %all-to-all-start.2 = ((bf16[512,16,256]{0,2,1:T(8,128)(2,1)}), bf16[512,16,256]{0,2,1:T(8,128)(2,1)}, u32[]{:S(2)}, u32[]{:S(2)}) async-start(bf16[512,16,256]{0,2,1:T(8,128)(2,1)} %select_select_fusion), calls=%async_computation.4 | async-start | bytes 8388608 | tf_op jit(solution)/shard_map/all_to_all | solution.py:106
  342.2 95.9 %all-to-all-done.2 = bf16[512,16,256]{0,2,1:T(8,128)(2,1)} async-done(((bf16[512,16,256]{0,2,1:T(8,128)(2,1)}), bf16[512,16,256]{0,2,1:T(8,128)(2,1)}, u32[]{:S(2)}, u32[]{:S(2)}) %all-to-all-start.2) | async-done | bytes 4194336 | tf_op jit(solution)/shard_map/all_to_all | solution.py:106
  438.1 6.4 %copy.22 = bf16[16,512,1,256]{3,1,0,2:T(8,128)(2,1)} copy(bf16[16,512,1,256]{1,3,0,2:T(8,128)(2,1)} %bitcast.18) | data formatting | bytes 8388608 | tf_op jit(solution)/shard_map/all_to_all | solution.py:106
  444.5 3.0 copy.26
  (18 shorter events, 0.2 us)
Async XLA Ops:
  7.2 161.4 %all-gather.4.cloned.1.call-start = ((), (), s32[]{:S(2)}) async-start(), calls=%async_computation.5 | async-start | bytes 17825792 | tf_op jit(solution)/shard_map/all_gather | solution.py:87
  7.9 213.8 %reduce-scatter.3.cloned.1.call-start = ((), (), s32[]{:S(2)}) async-start(), calls=%async_computation.6 | async-start | bytes 2359296 | tf_op jit(solution)/shard_map/reduce_scatter | solution.py:23
  177.6 62.7 %copy-start = (f32[512,128]{1,0:T(8,128)S(1)}, f32[512,128]{1,0:T(8,128)}, u32[]{:S(2)}) copy-start(f32[512,128]{1,0:T(8,128)} %param.9) | copy-start | bytes 786436
  177.6 62.7 %copy-start.1 = (f32[512,128]{1,0:T(8,128)S(1)}, f32[512,128]{1,0:T(8,128)}, u32[]{:S(2)}) copy-start(f32[512,128]{1,0:T(8,128)} %param.11) | copy-start | bytes 786436
  177.6 62.7 %copy-start.2 = (f32[512,128]{1,0:T(8,128)S(1)}, f32[512,128]{1,0:T(8,128)}, u32[]{:S(2)}) copy-start(f32[512,128]{1,0:T(8,128)} %param.10) | copy-start | bytes 786436
  180.7 59.6 %reduce-scatter.5.cloned.1.call-start = ((), (), s32[]{:S(2)}) async-start(), calls=%async_computation.7 | async-start | bytes 393216 | tf_op jit(solution)/shard_map/reduce_scatter | solution.py:23
  221.7 83.8 %all-gather.6.cloned.1.call-start = ((), (), s32[]{:S(2)}) async-start(), calls=%async_computation.8 | async-start | bytes 2228224 | tf_op jit(solution)/shard_map/all_gather | solution.py:96
  244.9 86.1 %all-to-all-start.1 = ((bf16[16,512,128]{2,1,0:T(8,128)(2,1)}), bf16[16,512,128]{2,1,0:T(8,128)(2,1)}, u32[]{:S(2)}, u32[]{:S(2)}) async-start(bf16[16,512,128]{2,1,0:T(8,128)(2,1)} %broadcast_in_dim.78), calls=%async_computation.3 | async-start | bytes 4194304 | tf_op jit(solution)/shard_map/all_to_all | solution.py:39
  331.0 107.1 %all-to-all-start.2 = ((bf16[512,16,256]{0,2,1:T(8,128)(2,1)}), bf16[512,16,256]{0,2,1:T(8,128)(2,1)}, u32[]{:S(2)}, u32[]{:S(2)}) async-start(bf16[512,16,256]{0,2,1:T(8,128)(2,1)} %select_select_fusion), calls=%async_computation.4 | async-start | bytes 8388608 | tf_op jit(solution)/shard_map/all_to_all | solution.py:106
Sparse Core Ops, SparseCore 0:
  10.5 158.0 all-gather.3
  180.8 40.8 reduce-scatter.2
  224.2 16.0 reduce-scatter.4
  243.4 62.0 all-gather.5
